TPU v7x, 32 devices: a whole 2x2x4 slice. The times are simulated.
32 devices in a mesh: sector: 16 (over z, y, x), op: 2 (over core).
Axes of the slice: x: 2, y: 2, z: 4, core: 2. Of those that a mesh axis runs over, the one named last changes fastest.
Arguments:
- wave_start: float32 [32, 256, 256], P('sector'), may hold values from -6 to 6
- left_blocks: float32 [4, 32, 256, 256], P('op', 'sector'), may hold values from -0.375 to 0.375
- right_blocks: float32 [4, 32, 256, 256], P('op', 'sector'), may hold values from -0.1875 to 0.1875
- term_shifts: int32 [4], P('op'), may hold values from -1 to 1
- preconditioner: float32 [32, 256, 256], P('sector'), may hold values from 0.5 to 4
Outputs:
- basis: float32 [3, 32, 256, 256], P(None, 'sector', 'op')
- ritz: float32 [3], replicated
Inputs may be any that keep to these rules, and one draw needn't show every extreme that they name: Each term changes the charge sector by term_shifts, one of -1, 0 and 1.
All inputs are finite; a program needn't handle non-finite values.
Results may differ from a plain program's by a relative error of at most 0.0003.
Values sent between devices are 32-bit elements; how exact they have to be, the bound alone decides.
No kernel may reach another device: no remote copies, remote signals or barrier semaphores. Data moves between devices by JAX's collectives and lax.ppermute only.
A program may use at most 64 MiB of HBM per device.

v0:
```python
import jax
import jax.numpy as jnp
from jax import lax
from jax.sharding import PartitionSpec as P

ITERS = 3
EPSILON = 1e-06


def with_halo(cells, sides, width):
    for axis, dim in sides:
        count = lax.axis_size(axis)
        ends = count - 1
        head = lax.slice_in_dim(cells, 0, width, axis=dim)
        tail = lax.slice_in_dim(cells, cells.shape[dim] - width, cells.shape[dim], axis=dim)
        cells = jnp.concatenate(
            [
                lax.ppermute(tail, axis, [(i, (i + 1) % count) for i in range(ends)]),
                cells,
                lax.ppermute(head, axis, [((i + 1) % count, i) for i in range(ends)]),
            ],
            axis=dim,
        )
    return cells


def body(wave_start, left_blocks, right_blocks, term_shifts, preconditioner):
    highest = lax.Precision.HIGHEST
    width = wave_start.shape[1]
    row_count = width // lax.axis_size("op")
    first_row = lax.axis_index("op") * row_count
    total = float(wave_start.shape[0] * lax.axis_size("sector") * width * wave_start.shape[2])

    def own_rows(values):
        return lax.dynamic_slice_in_dim(values, first_row, row_count, axis=values.ndim - 2)

    def portion(values):
        return own_rows(values)

    start_sum = lax.psum(jnp.sum(jnp.square(portion(wave_start))), ("sector", "op")) / total
    factor = lax.rsqrt(start_sum + EPSILON)
    applied = wave_start * factor
    basis = [wave_start * factor]
    ritz = []
    for index in range(ITERS):
        latest = basis[-1]
        padded = with_halo(applied, (("sector", 0),), 1)
        shift = term_shifts[:, None, None, None]
        source = jnp.where(
            shift == 1,
            padded[None, :-2],
            jnp.where(shift == -1, padded[None, 2:], padded[None, 1:-1]),
        )
        inner = jnp.einsum("ksab,ksbc->ksac", left_blocks, source, precision=highest)
        image = lax.psum(jnp.einsum("ksac,kscd->sad", inner, right_blocks, precision=highest), "op")
        ratio_image = image / preconditioner
        ratio_basis = latest / preconditioner
        part_image = portion(ratio_image)
        part_basis = portion(ratio_basis)
        pieces = [
            jnp.sum(portion(latest) * portion(image)),
            jnp.sum(part_image * part_image),
            jnp.sum(part_image * part_basis),
            jnp.sum(part_basis * part_basis),
        ]
        pieces = pieces + [jnp.sum(portion(member) * part_image) for member in basis]
        pieces = pieces + [jnp.sum(portion(member) * part_basis) for member in basis]
        sums = lax.psum(jnp.stack(pieces), ("sector", "op")) / total
        count = len(basis)
        theta = sums[0]
        correlations = sums[4 : 4 + count] - theta * sums[4 + count :]
        correction = ratio_image - theta * ratio_basis
        ortho = correction
        for position, member in enumerate(basis):
            ortho = ortho - correlations[position] * member
        length = (
            sums[1]
            - 2.0 * theta * sums[2]
            + theta * theta * sums[3]
            - jnp.sum(jnp.square(correlations))
        )
        fresh = ortho * lax.rsqrt(length + EPSILON)
        basis.append(fresh)
        ritz.append(theta)
        if index + 1 < ITERS:
            applied = fresh
    output = jnp.stack([portion(member) for member in basis[1:]])
    return (output, jnp.stack(ritz))


def solution(mesh):
    placed = (
        P("sector", None, None),
        P("op", "sector", None, None),
        P("op", "sector", None, None),
        P("op"),
        P("sector", None, None),
    )
    return jax.shard_map(
        body,
        mesh=mesh,
        in_specs=placed,
        out_specs=(P(None, "sector", "op", None), P()),
        check_vma=False,
    )
```

profile of v0, /device:TPU:0, one launch (start us, length us, event | category | flops | bytes accessed | tf_op | source)
XLA Modules:
  0.0 348.4 jit_solution(17925297234444958489)
XLA Ops:
  7.2 0.0 copy-start
  7.2 0.0 all-reduce.4.cloned.1.call-start
  7.2 1.7 multiply_reduce_fusion.24
  8.9 42.2 %psum.49 = f32[]{:T(128)} all-reduce(f32[]{:T(128)} %multiply_reduce_fusion.24), channel_id=1, replica_groups=mesh['sector'=16,'op'=2] {'sector','op'}, use_global_device_ids=true, to_apply=%region_1.0 | all-reduce | flops 1 | bytes 8 | tf_op jit(solution)/shard_map/psum | solution.py:40
  51.8 1.3 fusion.11
  53.2 0.0 copy-start.16
  53.2 4.3 %collective-permute-start = (f32[1,256,256]{2,1,0:T(8,128)S(1)}, f32[1,256,256]{2,1,0:T(8,128)S(1)}, u32[]{:S(2)}, u32[]{:S(2)}) collective-permute-start(f32[1,256,256]{2,1,0:T(8,128)S(1)} %get-tuple-element.48), channel_id=1, source_target_pairs={{0,2},{2,4},{4,6},{6,8},{8,10},{10,12},{12,14},{14,16},{16,18},{18... | collective-permute-start | bytes 786440 | tf_op jit(solution)/shard_map/ppermute | solution.py:18
  57.5 1.3 collective-permute-start.1
  58.8 8.3 %collective-permute-done = f32[1,256,256]{2,1,0:T(8,128)S(1)} collective-permute-done((f32[1,256,256]{2,1,0:T(8,128)S(1)}, f32[1,256,256]{2,1,0:T(8,128)S(1)}, u32[]{:S(2)}, u32[]{:S(2)}) %collective-permute-start) | collective-permute-done | bytes 262176 | tf_op jit(solution)/shard_map/ppermute | solution.py:18
  67.2 1.9 collective-permute-done.1
  69.0 0.1 pad_maximum_fusion.6
  69.1 0.0 copy-start.2
  69.2 1.4 convolution_bitcast_fusion.2
  70.5 2.0 convolution_bitcast_fusion.5
  72.5 0.0 all-reduce.4.cloned.1.call-update
  72.5 0.0 all-reduce.6.cloned.1.call-start
  72.5 17.9 %all-reduce.4.cloned.1.call-done = f32[2,256,256]{2,1,0:T(8,128)} async-done(((f32[2,256,256]{2,1,0:T(8,128)}), f32[2,256,256]{2,1,0:T(8,128)}) %all-reduce.4.cloned.1.call-update) | async-done | bytes 524304 | tf_op jit(solution)/shard_map/psum | solution.py:55
  90.5 1.2 div.31
  91.7 0.0 copy-start.8
  91.7 0.8 multiply_reduce_fusion.18
  92.5 3.8 %stack.102 = f32[6]{0:T(128)S(1)} concatenate(f32[1]{0:T(128)} %bitcast.3, f32[1]{0:T(128)} %bitcast.4, f32[1]{0:T(128)} %bitcast.5, f32[1]{0:T(128)} %bitcast.6, f32[1]{0:T(128)} %bitcast.7, f32[1]{0:T(128)} %bitcast.8), dimensions={0} | concatenate | bytes 48 | tf_op jit(solution)/shard_map/stack | solution.py:68
  96.3 40.5 %psum.51 = f32[6]{0:T(128)S(1)} all-reduce(f32[6]{0:T(128)S(1)} %stack.102), channel_id=1, replica_groups=mesh['sector'=16,'op'=2] {'sector','op'}, use_global_device_ids=true, to_apply=%region_9.10 | all-reduce | flops 6 | bytes 48 | tf_op jit(solution)/shard_map/psum | solution.py:68
  136.8 0.7 fusion.19
  143.4 2.0 fusion.10
  145.5 4.2 %collective-permute-start.2 = (f32[1,256,256]{2,1,0:T(8,128)S(1)}, f32[1,256,256]{2,1,0:T(8,128)S(1)}, u32[]{:S(2)}, u32[]{:S(2)}) collective-permute-start(f32[1,256,256]{2,1,0:T(8,128)S(1)} %get-tuple-element.44), channel_id=1, source_target_pairs={{0,2},{2,4},{4,6},{6,8},{8,10},{10,12},{12,14},{14,16},{16,18},{18... | collective-permute-start | bytes 786440 | tf_op jit(solution)/shard_map/ppermute | solution.py:18
  149.7 1.3 collective-permute-start.3
  151.0 8.2 %collective-permute-done.2 = f32[1,256,256]{2,1,0:T(8,128)S(1)} collective-permute-done((f32[1,256,256]{2,1,0:T(8,128)S(1)}, f32[1,256,256]{2,1,0:T(8,128)S(1)}, u32[]{:S(2)}, u32[]{:S(2)}) %collective-permute-start.2) | collective-permute-done | bytes 262176 | tf_op jit(solution)/shard_map/ppermute | solution.py:18
  159.3 1.8 collective-permute-done.3
  161.1 0.1 pad_maximum_fusion.4
  161.1 0.0 copy-start.3
  161.2 1.4 convolution_bitcast_fusion.1
  162.5 1.9 convolution_bitcast_fusion.4
  164.5 0.0 all-reduce.6.cloned.1.call-update
  164.5 0.0 all-reduce.8.cloned.1.call-start
  164.5 18.0 %all-reduce.6.cloned.1.call-done = f32[2,256,256]{2,1,0:T(8,128)} async-done(((f32[2,256,256]{2,1,0:T(8,128)}), f32[2,256,256]{2,1,0:T(8,128)}) %all-reduce.6.cloned.1.call-update) | async-done | bytes 524304 | tf_op jit(solution)/shard_map/psum | solution.py:55
  182.5 1.2 div.34
  183.7 0.0 copy-start.7
  183.7 0.9 multiply_reduce_fusion.10
  184.6 5.1 %stack.112 = f32[8]{0:T(128)S(1)} concatenate(f32[1]{0:T(128)} %bitcast.19, f32[1]{0:T(128)} %bitcast.20, f32[1]{0:T(128)} %bitcast.21, f32[1]{0:T(128)} %bitcast.22, f32[1]{0:T(128)} %bitcast.23, f32[1]{0:T(128)} %bitcast.24, f32[1]{0:T(128)} %bitcast.25, f32[1]{0:T(128)} %bitcast.26), dimensions={0} | concatenate | bytes 64 | tf_op jit(solution)/shard_map/stack | solution.py:68
  189.8 40.5 %psum.53 = f32[8]{0:T(128)S(1)} all-reduce(f32[8]{0:T(128)S(1)} %stack.112), channel_id=1, replica_groups=mesh['sector'=16,'op'=2] {'sector','op'}, use_global_device_ids=true, to_apply=%region_19.20 | all-reduce | flops 8 | bytes 64 | tf_op jit(solution)/shard_map/psum | solution.py:68
  230.3 0.7 fusion.18
  232.6 1.3 multiply_reduce_fusion.26
  236.5 0.7 fusion.17
  237.2 4.1 %fusion.9 = (f32[2,256,256]{2,1,0:T(8,128)}, f32[2,256,256]{2,1,0:T(8,128)S(1)}) fusion(f32[2,256,256]{2,1,0:T(8,128)S(1)} %copy-done.1, f32[]{:T(128)S(6)} %rsqrt.14, f32[2,256,256]{2,1,0:T(8,128)S(1)} %get-tuple-element.33, f32[]{:T(128)} %bitcast.29, f32[2,256,256]{2,1,0:T(8,128)S(1)} %get-tuple-element.35, f32[]{:T(128)} %bitcast.28, ...), kind=kLoop, calls=%fused_computation.66 | loop fusion | flops 1048576 | bytes 3670032 | tf_op jit(solution)/shard_map/div | solution.py:57
  241.3 4.2 %collective-permute-start.4 = (f32[1,256,256]{2,1,0:T(8,128)S(1)}, f32[1,256,256]{2,1,0:T(8,128)S(1)}, u32[]{:S(2)}, u32[]{:S(2)}) collective-permute-start(f32[1,256,256]{2,1,0:T(8,128)S(1)} %get-tuple-element.40), channel_id=1, source_target_pairs={{0,2},{2,4},{4,6},{6,8},{8,10},{10,12},{12,14},{14,16},{16,18},{18... | collective-permute-start | bytes 786440 | tf_op jit(solution)/shard_map/ppermute | solution.py:18
  245.5 1.5 collective-permute-start.5
  247.0 8.0 %collective-permute-done.4 = f32[1,256,256]{2,1,0:T(8,128)S(1)} collective-permute-done((f32[1,256,256]{2,1,0:T(8,128)S(1)}, f32[1,256,256]{2,1,0:T(8,128)S(1)}, u32[]{:S(2)}, u32[]{:S(2)}) %collective-permute-start.4) | collective-permute-done | bytes 262176 | tf_op jit(solution)/shard_map/ppermute | solution.py:18
  255.0 1.8 collective-permute-done.5
  256.8 0.1 pad_maximum_fusion.2
  256.9 1.4 convolution_bitcast_fusion
  258.3 1.9 convolution_bitcast_fusion.3
  260.2 0.0 all-reduce.8.cloned.1.call-update
  260.2 18.0 %all-reduce.8.cloned.1.call-done = f32[2,256,256]{2,1,0:T(8,128)} async-done(((f32[2,256,256]{2,1,0:T(8,128)}), f32[2,256,256]{2,1,0:T(8,128)}) %all-reduce.8.cloned.1.call-update) | async-done | bytes 524304 | tf_op jit(solution)/shard_map/psum | solution.py:55
  278.3 1.2 div.37
  279.5 0.1 copy-done.12
  279.6 1.5 multiply_reduce_fusion
  281.1 6.2 %stack.124 = f32[10]{0:T(128)S(1)} concatenate(f32[1]{0:T(128)} %bitcast.37, f32[1]{0:T(128)} %bitcast.38, f32[1]{0:T(128)} %bitcast.39, f32[1]{0:T(128)} %bitcast.40, f32[1]{0:T(128)} %bitcast.41, f32[1]{0:T(128)} %bitcast.42, f32[1]{0:T(128)} %bitcast.43, f32[1]{0:T(128)} %bitcast.44, f32[1]{0:T(128)} %bitcast.45, f32[1]{0:T(128)} %bitcast.46), dimensions={0} | concatenate | bytes 80 | tf_op jit(solution)/shard_map/stack | solution.py:68
  287.4 40.5 %psum.55 = f32[10]{0:T(128)S(1)} all-reduce(f32[10]{0:T(128)S(1)} %stack.124), channel_id=1, replica_groups=mesh['sector'=16,'op'=2] {'sector','op'}, use_global_device_ids=true, to_apply=%region_32.33 | all-reduce | flops 10 | bytes 80 | tf_op jit(solution)/shard_map/psum | solution.py:68
  327.9 0.7 fusion.16
  330.5 2.5 pad_maximum_fusion.7
  332.9 1.3 multiply_reduce_fusion.25
  336.7 0.7 fusion.15
  337.4 3.5 %multiply_bitcast_fusion = f32[1,2,128,256]{3,2,1,0:T(8,128)S(1)} fusion(f32[2,256,256]{2,1,0:T(8,128)S(1)} %get-tuple-element.29, s32[]{:T(128)S(6)} %select_n.22, f32[2,256,256]{2,1,0:T(8,128)} %copy-done.11, f32[2,256,256]{2,1,0:T(8,128)S(1)} %copy-done.10, f32[2,256,256]{2,1,0:T(8,128)S(1)} %get-tuple-element.33, ...), kind=kLoop, calls=%fused_computation.27 | loop fusion | flops 589824 | bytes 1572888 | tf_op jit(solution)/shard_map/stack | solution.py:87
  340.9 0.9 pad_maximum_fusion
  (34 shorter events, 0.2 us)
Async XLA Ops:
  7.2 62.0 %copy-start = (f32[2,2,256,256]{3,2,1,0:T(8,128)S(1)}, f32[2,2,256,256]{3,2,1,0:T(8,128)}, u32[]{:S(2)}) copy-start(f32[2,2,256,256]{3,2,1,0:T(8,128)} %param.6) | copy-start | bytes 3145732
  7.2 83.3 %all-reduce.4.cloned.1.call-start = ((), (), s32[]{:S(2)}) async-start(), calls=%async_computation | async-start | bytes 1048576 | tf_op jit(solution)/shard_map/psum | solution.py:55
  53.1 38.6 %copy-start.6 = (f32[2,256,256]{2,1,0:T(8,128)}, f32[2,256,256]{2,1,0:T(8,128)S(1)}, u32[]{:S(2)}) copy-start(f32[2,256,256]{2,1,0:T(8,128)S(1)} %get-tuple-element.34) | copy-start | bytes 1572868
  53.2 5.6 %copy-start.16 = (s32[2]{0:T(128)S(1)}, s32[2]{0:T(128)}, u32[]{:S(2)}) copy-start(s32[2]{0:T(128)} %param.8) | copy-start | bytes 28
  53.2 14.0 %collective-permute-start = (f32[1,256,256]{2,1,0:T(8,128)S(1)}, f32[1,256,256]{2,1,0:T(8,128)S(1)}, u32[]{:S(2)}, u32[]{:S(2)}) collective-permute-start(f32[1,256,256]{2,1,0:T(8,128)S(1)} %get-tuple-element.48), channel_id=1, source_target_pairs={{0,2},{2,4},{4,6},{6,8},{8,10},{10,12},{12,14},{14,16},{16,18},{18... | collective-permute-start | bytes 786440 | tf_op jit(solution)/shard_map/ppermute | solution.py:18
  57.5 11.5 %collective-permute-start.1 = (f32[1,256,256]{2,1,0:T(8,128)S(1)}, f32[1,256,256]{2,1,0:T(8,128)S(1)}, u32[]{:S(2)}, u32[]{:S(2)}) collective-permute-start(f32[1,256,256]{2,1,0:T(8,128)S(1)} %get-tuple-element.49), channel_id=1, source_target_pairs={{2,0},{4,2},{6,4},{8,6},{10,8},{12,10},{14,12},{16,14},{18,16},{20... | collective-permute-start | bytes 786440 | tf_op jit(solution)/shard_map/ppermute | solution.py:20
  69.1 1.4 copy-start.2
  72.5 18.0 %copy-start.1 = (f32[2,256,256]{2,1,0:T(8,128)S(1)}, f32[2,256,256]{2,1,0:T(8,128)}, u32[]{:S(2)}) copy-start(f32[2,256,256]{2,1,0:T(8,128)} %param.9) | copy-start | bytes 1572868
  72.5 110.0 %all-reduce.6.cloned.1.call-start = ((), (), s32[]{:S(2)}) async-start(), calls=%async_computation.1 | async-start | bytes 1048576 | tf_op jit(solution)/shard_map/psum | solution.py:55
  90.5 1.2 copy-start.14
  91.7 0.8 copy-start.8
  145.5 38.2 %copy-start.5 = (f32[2,256,256]{2,1,0:T(8,128)}, f32[2,256,256]{2,1,0:T(8,128)S(1)}, u32[]{:S(2)}) copy-start(f32[2,256,256]{2,1,0:T(8,128)S(1)} %get-tuple-element.32) | copy-start | bytes 1572868
  145.5 13.7 %collective-permute-start.2 = (f32[1,256,256]{2,1,0:T(8,128)S(1)}, f32[1,256,256]{2,1,0:T(8,128)S(1)}, u32[]{:S(2)}, u32[]{:S(2)}) collective-permute-start(f32[1,256,256]{2,1,0:T(8,128)S(1)} %get-tuple-element.44), channel_id=1, source_target_pairs={{0,2},{2,4},{4,6},{6,8},{8,10},{10,12},{12,14},{14,16},{16,18},{18... | collective-permute-start | bytes 786440 | tf_op jit(solution)/shard_map/ppermute | solution.py:18
  149.7 11.3 %collective-permute-start.3 = (f32[1,256,256]{2,1,0:T(8,128)S(1)}, f32[1,256,256]{2,1,0:T(8,128)S(1)}, u32[]{:S(2)}, u32[]{:S(2)}) collective-permute-start(f32[1,256,256]{2,1,0:T(8,128)S(1)} %get-tuple-element.45), channel_id=1, source_target_pairs={{2,0},{4,2},{6,4},{8,6},{10,8},{12,10},{14,12},{16,14},{18,16},{20... | collective-permute-start | bytes 786440 | tf_op jit(solution)/shard_map/ppermute | solution.py:20
  161.1 1.4 copy-start.3
  164.5 113.8 %all-reduce.8.cloned.1.call-start = ((), (), s32[]{:S(2)}) async-start(), calls=%async_computation.2 | async-start | bytes 1048576 | tf_op jit(solution)/shard_map/psum | solution.py:55
  182.5 1.2 copy-start.13
  183.7 0.9 copy-start.7
  241.3 13.7 %collective-permute-start.4 = (f32[1,256,256]{2,1,0:T(8,128)S(1)}, f32[1,256,256]{2,1,0:T(8,128)S(1)}, u32[]{:S(2)}, u32[]{:S(2)}) collective-permute-start(f32[1,256,256]{2,1,0:T(8,128)S(1)} %get-tuple-element.40), channel_id=1, source_target_pairs={{0,2},{2,4},{4,6},{6,8},{8,10},{10,12},{12,14},{14,16},{16,18},{18... | collective-permute-start | bytes 786440 | tf_op jit(solution)/shard_map/ppermute | solution.py:18
  245.5 11.3 %collective-permute-start.5 = (f32[1,256,256]{2,1,0:T(8,128)S(1)}, f32[1,256,256]{2,1,0:T(8,128)S(1)}, u32[]{:S(2)}, u32[]{:S(2)}) collective-permute-start(f32[1,256,256]{2,1,0:T(8,128)S(1)} %get-tuple-element.41), channel_id=1, source_target_pairs={{2,0},{4,2},{6,4},{8,6},{10,8},{12,10},{14,12},{16,14},{18,16},{20... | collective-permute-start | bytes 786440 | tf_op jit(solution)/shard_map/ppermute | solution.py:20
  256.9 1.4 copy-start.4
  278.2 1.2 copy-start.9
  278.2 1.4 copy-start.12
  279.5 1.7 copy-start.11
  279.6 57.8 %copy-start.10 = (f32[2,256,256]{2,1,0:T(8,128)S(1)}, f32[2,256,256]{2,1,0:T(8,128)}, u32[]{:S(2)}) copy-start(f32[2,256,256]{2,1,0:T(8,128)} %get-tuple-element.28) | copy-start | bytes 1572868
  337.4 3.5 %copy-start.15 = (f32[1,2,128,256]{3,2,1,0:T(8,128)S(1)}, f32[1,2,128,256]{3,2,1,0:T(8,128)}, u32[]{:S(2)}) copy-start(f32[1,2,128,256]{3,2,1,0:T(8,128)} %get-tuple-element.37) | copy-start | bytes 786436
Sparse Core Ops, SparseCore 0:
  72.6 17.8 all-reduce.3
  164.6 17.8 all-reduce.5
  260.4 17.8 all-reduce.7
where the time goes:
time: 350 us; the launch traced here: 348 us
  blocking collectives  164 us (47%)
  waiting for transfers between devices  84 us (24%)
  between operations  29.4 us (8%)
  other arithmetic  25.7 us (7%)
  local copies, waits for them, and re-layouts  18.8 us (5%)
  starting transfers between devices  16.9 us (5%)
  matrix products  9.9 us (3%)
    psum x3, blocking collectives, body(): sums = lax.psum(jnp.stack(pieces), ('sector', 'op')) / total  122 us
    psum x3, waiting for transfers between devices, body(): lax.psum(jnp.einsum('ksac,kscd->sad', inner, right_blocks, precision=high...  53.9 us
    psum x1, blocking collectives, body(): lax.psum(jnp.sum(jnp.square(portion(wave_start))), ('sector', 'op')) / total  42.2 us
    ppermute x3, waiting for transfers between devices, with_halo(): lax.ppermute(tail, axis, [(i, (i + 1) % count) for i in range(ends)])  24.5 us
    another operation x3, local copies, waits for them, and re-layouts, body(): sums = lax.psum(jnp.stack(pieces), ('sector', 'op')) / total  15.2 us
    ppermute x3, starting transfers between devices, with_halo(): lax.ppermute(tail, axis, [(i, (i + 1) % count) for i in range(ends)])  12.7 us
    div x3, other arithmetic, body(): ratio_basis = latest / preconditioner  7.41 us
  transfers between devices with their start and end apart: 9, of which 9 were waited for; matrix products, arithmetic and copies ran while one was open for 0% of the time, Pallas kernels for 0%

commit v1 on v0

--- a/solution.py
+++ b/solution.py
@@ -5,6 +5,12 @@
 
 ITERS = 3
 EPSILON = 1e-06
+
+
+def gather_and_add(value, axis):
+    parts = lax.all_gather(value, axis, axis=0, tiled=False)
+    total = parts.sum(axis=0)
+    return total
 
 
 def with_halo(cells, sides, width):
@@ -52,7 +58,9 @@
             jnp.where(shift == -1, padded[None, 2:], padded[None, 1:-1]),
         )
         inner = jnp.einsum("ksab,ksbc->ksac", left_blocks, source, precision=highest)
-        image = lax.psum(jnp.einsum("ksac,kscd->sad", inner, right_blocks, precision=highest), "op")
+        image = gather_and_add(
+            jnp.einsum("ksac,kscd->sad", inner, right_blocks, precision=highest), "op"
+        )
         ratio_image = image / preconditioner
         ratio_basis = latest / preconditioner
         part_image = portion(ratio_image)

time: 350 us -> 327 us (0.934)
  waiting for transfers between devices: 84 us -> 54.9 us
  other arithmetic: 25.7 us -> 32.2 us
    psum x3 -> x0, waiting for transfers between devices: 53.9 us -> none  [body(): lax.psum(jnp.einsum('ksac,kscd->sad', inner, right_blocks, precision=high...]
    all_gather x0 -> x3, waiting for transfers between devices: none -> 24.8 us  [gather_and_add(): parts = lax.all_gather(value, axis, axis=0, tiled=False)]
    reduce_sum x0 -> x3, other arithmetic: none -> 6.5 us  [gather_and_add(): total = parts.sum(axis=0)]
where the time goes in v1:
time: 327 us; the launch traced here: 326 us
  blocking collectives  164 us (50%)
  waiting for transfers between devices  54.9 us (17%)
  other arithmetic  32.2 us (10%)
  between operations  29.3 us (9%)
  local copies, waits for them, and re-layouts  18.9 us (6%)
  starting transfers between devices  16.9 us (5%)
  matrix products  9.93 us (3%)
    psum x3, blocking collectives, body(): sums = lax.psum(jnp.stack(pieces), ('sector', 'op')) / total  121 us
    psum x1, blocking collectives, body(): lax.psum(jnp.sum(jnp.square(portion(wave_start))), ('sector', 'op')) / total  42.2 us
    all_gather x3, waiting for transfers between devices, gather_and_add(): parts = lax.all_gather(value, axis, axis=0, tiled=False)  24.8 us
    ppermute x3, waiting for transfers between devices, with_halo(): lax.ppermute(tail, axis, [(i, (i + 1) % count) for i in range(ends)])  24.5 us
    another operation x3, local copies, waits for them, and re-layouts, body(): sums = lax.psum(jnp.stack(pieces), ('sector', 'op')) / total  15.2 us
    ppermute x3, starting transfers between devices, with_halo(): lax.ppermute(tail, axis, [(i, (i + 1) % count) for i in range(ends)])  12.7 us
    div x3, other arithmetic, body(): ratio_basis = latest / preconditioner  7.41 us
  transfers between devices with their start and end apart: 9, of which 9 were waited for; matrix products, arithmetic and copies ran while one was open for 0% of the time, Pallas kernels for 0%

profile of v1, /device:TPU:0, one launch (start us, length us, event | category | flops | bytes accessed | tf_op | source)
XLA Modules:
  0.0 325.8 jit_solution(13248368565301580009)
XLA Ops:
  7.2 0.0 copy-start
  7.2 0.0 all-gather.7.cloned.1.call-start
  7.2 1.7 multiply_reduce_fusion.24
  8.9 42.2 %psum.28 = f32[]{:T(128)} all-reduce(f32[]{:T(128)} %multiply_reduce_fusion.24), channel_id=1, replica_groups=mesh['sector'=16,'op'=2] {'sector','op'}, use_global_device_ids=true, to_apply=%region_1.0 | all-reduce | flops 1 | bytes 8 | tf_op jit(solution)/shard_map/psum | solution.py:46
  51.8 1.3 fusion.11
  53.2 0.0 copy-start.16
  53.2 4.3 %collective-permute-start = (f32[1,256,256]{2,1,0:T(8,128)S(1)}, f32[1,256,256]{2,1,0:T(8,128)S(1)}, u32[]{:S(2)}, u32[]{:S(2)}) collective-permute-start(f32[1,256,256]{2,1,0:T(8,128)S(1)} %get-tuple-element.48), channel_id=1, source_target_pairs={{0,2},{2,4},{4,6},{6,8},{8,10},{10,12},{12,14},{14,16},{16,18},{18... | collective-permute-start | bytes 786440 | tf_op jit(solution)/shard_map/ppermute | solution.py:24
  57.5 1.3 collective-permute-start.1
  58.8 8.3 %collective-permute-done = f32[1,256,256]{2,1,0:T(8,128)S(1)} collective-permute-done((f32[1,256,256]{2,1,0:T(8,128)S(1)}, f32[1,256,256]{2,1,0:T(8,128)S(1)}, u32[]{:S(2)}, u32[]{:S(2)}) %collective-permute-start) | collective-permute-done | bytes 262176 | tf_op jit(solution)/shard_map/ppermute | solution.py:24
  67.2 1.9 collective-permute-done.1
  69.0 0.1 pad_maximum_fusion.6
  69.1 0.0 copy-start.2
  69.1 1.4 convolution_bitcast_fusion.2
  70.5 2.0 convolution_bitcast_fusion.5
  72.5 0.0 all-gather.7.cloned.1.call-update
  72.5 0.0 all-gather.9.cloned.1.call-start
  72.5 8.2 %all-gather.7.cloned.1.call-done = f32[4,256,256]{2,1,0:T(8,128)} async-done(((f32[2,256,256]{2,1,0:T(8,128)}), f32[4,256,256]{2,1,0:T(8,128)}) %all-gather.7.cloned.1.call-update) | async-done | bytes 1048592 | tf_op jit(solution)/shard_map/all_gather | solution.py:11
  80.8 2.2 reduce_sum.277
  83.0 1.2 div.31
  84.2 0.8 multiply_reduce_fusion.18
  85.0 3.9 %stack.102 = f32[6]{0:T(128)S(1)} concatenate(f32[1]{0:T(128)} %bitcast.4, f32[1]{0:T(128)} %bitcast.5, f32[1]{0:T(128)} %bitcast.6, f32[1]{0:T(128)} %bitcast.7, f32[1]{0:T(128)} %bitcast.8, f32[1]{0:T(128)} %bitcast.9), dimensions={0} | concatenate | bytes 48 | tf_op jit(solution)/shard_map/stack | solution.py:76
  88.9 40.5 %psum.29 = f32[6]{0:T(128)S(1)} all-reduce(f32[6]{0:T(128)S(1)} %stack.102), channel_id=1, replica_groups=mesh['sector'=16,'op'=2] {'sector','op'}, use_global_device_ids=true, to_apply=%region_9.10 | all-reduce | flops 6 | bytes 48 | tf_op jit(solution)/shard_map/psum | solution.py:76
  129.4 0.7 fusion.19
  135.7 2.0 fusion.10
  137.7 4.2 %collective-permute-start.2 = (f32[1,256,256]{2,1,0:T(8,128)S(1)}, f32[1,256,256]{2,1,0:T(8,128)S(1)}, u32[]{:S(2)}, u32[]{:S(2)}) collective-permute-start(f32[1,256,256]{2,1,0:T(8,128)S(1)} %get-tuple-element.44), channel_id=1, source_target_pairs={{0,2},{2,4},{4,6},{6,8},{8,10},{10,12},{12,14},{14,16},{16,18},{18... | collective-permute-start | bytes 786440 | tf_op jit(solution)/shard_map/ppermute | solution.py:24
  142.0 1.3 collective-permute-start.3
  143.3 8.2 %collective-permute-done.2 = f32[1,256,256]{2,1,0:T(8,128)S(1)} collective-permute-done((f32[1,256,256]{2,1,0:T(8,128)S(1)}, f32[1,256,256]{2,1,0:T(8,128)S(1)}, u32[]{:S(2)}, u32[]{:S(2)}) %collective-permute-start.2) | collective-permute-done | bytes 262176 | tf_op jit(solution)/shard_map/ppermute | solution.py:24
  151.5 1.8 collective-permute-done.3
  153.3 0.1 pad_maximum_fusion.4
  153.4 1.4 convolution_bitcast_fusion.1
  154.7 1.9 convolution_bitcast_fusion.4
  156.7 0.0 all-gather.9.cloned.1.call-update
  156.7 0.0 all-gather.11.cloned.1.call-start
  156.8 8.3 %all-gather.9.cloned.1.call-done = f32[4,256,256]{2,1,0:T(8,128)} async-done(((f32[2,256,256]{2,1,0:T(8,128)}), f32[4,256,256]{2,1,0:T(8,128)}) %all-gather.9.cloned.1.call-update) | async-done | bytes 1048592 | tf_op jit(solution)/shard_map/all_gather | solution.py:11
  165.0 2.1 reduce_sum.285
  167.2 1.2 div.34
  168.4 0.9 multiply_reduce_fusion.10
  169.3 5.1 %stack.112 = f32[8]{0:T(128)S(1)} concatenate(f32[1]{0:T(128)} %bitcast.21, f32[1]{0:T(128)} %bitcast.22, f32[1]{0:T(128)} %bitcast.23, f32[1]{0:T(128)} %bitcast.24, f32[1]{0:T(128)} %bitcast.25, f32[1]{0:T(128)} %bitcast.26, f32[1]{0:T(128)} %bitcast.27, f32[1]{0:T(128)} %bitcast.28), dimensions={0} | concatenate | bytes 64 | tf_op jit(solution)/shard_map/stack | solution.py:76
  174.4 40.5 %psum.30 = f32[8]{0:T(128)S(1)} all-reduce(f32[8]{0:T(128)S(1)} %stack.112), channel_id=1, replica_groups=mesh['sector'=16,'op'=2] {'sector','op'}, use_global_device_ids=true, to_apply=%region_19.20 | all-reduce | flops 8 | bytes 64 | tf_op jit(solution)/shard_map/psum | solution.py:76
  214.9 0.7 fusion.18
  217.5 1.3 multiply_reduce_fusion.26
  221.4 0.7 fusion.17
  222.0 4.2 %fusion.9 = (f32[2,256,256]{2,1,0:T(8,128)}, f32[2,256,256]{2,1,0:T(8,128)S(1)}) fusion(f32[2,256,256]{2,1,0:T(8,128)S(1)} %copy-done.1, f32[]{:T(128)S(6)} %rsqrt.14, f32[2,256,256]{2,1,0:T(8,128)S(1)} %get-tuple-element.33, f32[]{:T(128)} %bitcast.31, f32[2,256,256]{2,1,0:T(8,128)S(1)} %get-tuple-element.35, f32[]{:T(128)} %bitcast.30, ...), kind=kLoop, calls=%fused_computation.66 | loop fusion | flops 1048576 | bytes 3670032 | tf_op jit(solution)/shard_map/div | solution.py:65
  226.2 4.2 %collective-permute-start.4 = (f32[1,256,256]{2,1,0:T(8,128)S(1)}, f32[1,256,256]{2,1,0:T(8,128)S(1)}, u32[]{:S(2)}, u32[]{:S(2)}) collective-permute-start(f32[1,256,256]{2,1,0:T(8,128)S(1)} %get-tuple-element.40), channel_id=1, source_target_pairs={{0,2},{2,4},{4,6},{6,8},{8,10},{10,12},{12,14},{14,16},{16,18},{18... | collective-permute-start | bytes 786440 | tf_op jit(solution)/shard_map/ppermute | solution.py:24
  230.4 1.5 collective-permute-start.5
  231.9 8.0 %collective-permute-done.4 = f32[1,256,256]{2,1,0:T(8,128)S(1)} collective-permute-done((f32[1,256,256]{2,1,0:T(8,128)S(1)}, f32[1,256,256]{2,1,0:T(8,128)S(1)}, u32[]{:S(2)}, u32[]{:S(2)}) %collective-permute-start.4) | collective-permute-done | bytes 262176 | tf_op jit(solution)/shard_map/ppermute | solution.py:24
  239.9 1.8 collective-permute-done.5
  241.7 0.1 pad_maximum_fusion.2
  241.8 1.4 convolution_bitcast_fusion
  243.2 2.0 convolution_bitcast_fusion.3
  245.2 0.0 all-gather.11.cloned.1.call-update
  245.2 8.3 %all-gather.11.cloned.1.call-done = f32[4,256,256]{2,1,0:T(8,128)} async-done(((f32[2,256,256]{2,1,0:T(8,128)}), f32[4,256,256]{2,1,0:T(8,128)}) %all-gather.11.cloned.1.call-update) | async-done | bytes 1048592 | tf_op jit(solution)/shard_map/all_gather | solution.py:11
  253.5 2.2 reduce_sum.295
  255.7 1.2 div.37
  256.9 0.1 copy-done.12
  257.0 1.5 multiply_reduce_fusion
  258.5 6.2 %stack.124 = f32[10]{0:T(128)S(1)} concatenate(f32[1]{0:T(128)} %bitcast.40, f32[1]{0:T(128)} %bitcast.41, f32[1]{0:T(128)} %bitcast.42, f32[1]{0:T(128)} %bitcast.43, f32[1]{0:T(128)} %bitcast.44, f32[1]{0:T(128)} %bitcast.45, f32[1]{0:T(128)} %bitcast.46, f32[1]{0:T(128)} %bitcast.47, f32[1]{0:T(128)} %bitcast.48, f32[1]{0:T(128)} %bitcast.49), dimensions={0} | concatenate | bytes 80 | tf_op jit(solution)/shard_map/stack | solution.py:76
  264.8 40.5 %psum.31 = f32[10]{0:T(128)S(1)} all-reduce(f32[10]{0:T(128)S(1)} %stack.124), channel_id=1, replica_groups=mesh['sector'=16,'op'=2] {'sector','op'}, use_global_device_ids=true, to_apply=%region_32.33 | all-reduce | flops 10 | bytes 80 | tf_op jit(solution)/shard_map/psum | solution.py:76
  305.3 0.7 fusion.16
  307.9 2.5 pad_maximum_fusion.7
  310.3 1.3 multiply_reduce_fusion.25
  314.1 0.7 fusion.15
  314.8 3.5 %multiply_bitcast_fusion = f32[1,2,128,256]{3,2,1,0:T(8,128)S(1)} fusion(f32[2,256,256]{2,1,0:T(8,128)S(1)} %get-tuple-element.29, s32[]{:T(128)S(6)} %select_n.22, f32[2,256,256]{2,1,0:T(8,128)} %copy-done.14, f32[2,256,256]{2,1,0:T(8,128)S(1)} %copy-done.13, f32[2,256,256]{2,1,0:T(8,128)S(1)} %get-tuple-element.33, ...), kind=kLoop, calls=%fused_computation.27 | loop fusion | flops 589824 | bytes 1572888 | tf_op jit(solution)/shard_map/stack | solution.py:95
  318.3 0.9 pad_maximum_fusion
  (37 shorter events, 0.2 us)
Async XLA Ops:
  7.2 62.0 %copy-start = (f32[2,2,256,256]{3,2,1,0:T(8,128)S(1)}, f32[2,2,256,256]{3,2,1,0:T(8,128)}, u32[]{:S(2)}) copy-start(f32[2,2,256,256]{3,2,1,0:T(8,128)} %param.6) | copy-start | bytes 3145732
  7.2 73.6 %all-gather.7.cloned.1.call-start = ((), (), s32[]{:S(2)}) async-start(), calls=%async_computation | async-start | bytes 1572864 | tf_op jit(solution)/shard_map/all_gather | solution.py:11
  53.1 31.1 %copy-start.6 = (f32[2,256,256]{2,1,0:T(8,128)}, f32[2,256,256]{2,1,0:T(8,128)S(1)}, u32[]{:S(2)}) copy-start(f32[2,256,256]{2,1,0:T(8,128)S(1)} %get-tuple-element.34) | copy-start | bytes 1572868
  53.2 5.6 %copy-start.16 = (s32[2]{0:T(128)S(1)}, s32[2]{0:T(128)}, u32[]{:S(2)}) copy-start(s32[2]{0:T(128)} %param.8) | copy-start | bytes 28
  53.2 14.0 %collective-permute-start = (f32[1,256,256]{2,1,0:T(8,128)S(1)}, f32[1,256,256]{2,1,0:T(8,128)S(1)}, u32[]{:S(2)}, u32[]{:S(2)}) collective-permute-start(f32[1,256,256]{2,1,0:T(8,128)S(1)} %get-tuple-element.48), channel_id=1, source_target_pairs={{0,2},{2,4},{4,6},{6,8},{8,10},{10,12},{12,14},{14,16},{16,18},{18... | collective-permute-start | bytes 786440 | tf_op jit(solution)/shard_map/ppermute | solution.py:24
  57.5 11.5 %collective-permute-start.1 = (f32[1,256,256]{2,1,0:T(8,128)S(1)}, f32[1,256,256]{2,1,0:T(8,128)S(1)}, u32[]{:S(2)}, u32[]{:S(2)}) collective-permute-start(f32[1,256,256]{2,1,0:T(8,128)S(1)} %get-tuple-element.49), channel_id=1, source_target_pairs={{2,0},{4,2},{6,4},{8,6},{10,8},{12,10},{14,12},{16,14},{18,16},{20... | collective-permute-start | bytes 786440 | tf_op jit(solution)/shard_map/ppermute | solution.py:26
  69.1 1.4 copy-start.2
  72.5 92.5 %all-gather.9.cloned.1.call-start = ((), (), s32[]{:S(2)}) async-start(), calls=%async_computation.1 | async-start | bytes 1572864 | tf_op jit(solution)/shard_map/all_gather | solution.py:11
  80.8 2.2 copy-start.1
  83.0 1.2 copy-start.11
  84.2 0.9 copy-start.8
  137.7 30.7 %copy-start.5 = (f32[2,256,256]{2,1,0:T(8,128)}, f32[2,256,256]{2,1,0:T(8,128)S(1)}, u32[]{:S(2)}) copy-start(f32[2,256,256]{2,1,0:T(8,128)S(1)} %get-tuple-element.32) | copy-start | bytes 1572868
  137.7 13.7 %collective-permute-start.2 = (f32[1,256,256]{2,1,0:T(8,128)S(1)}, f32[1,256,256]{2,1,0:T(8,128)S(1)}, u32[]{:S(2)}, u32[]{:S(2)}) collective-permute-start(f32[1,256,256]{2,1,0:T(8,128)S(1)} %get-tuple-element.44), channel_id=1, source_target_pairs={{0,2},{2,4},{4,6},{6,8},{8,10},{10,12},{12,14},{14,16},{16,18},{18... | collective-permute-start | bytes 786440 | tf_op jit(solution)/shard_map/ppermute | solution.py:24
  142.0 11.3 %collective-permute-start.3 = (f32[1,256,256]{2,1,0:T(8,128)S(1)}, f32[1,256,256]{2,1,0:T(8,128)S(1)}, u32[]{:S(2)}, u32[]{:S(2)}) collective-permute-start(f32[1,256,256]{2,1,0:T(8,128)S(1)} %get-tuple-element.45), channel_id=1, source_target_pairs={{2,0},{4,2},{6,4},{8,6},{10,8},{12,10},{14,12},{16,14},{18,16},{20... | collective-permute-start | bytes 786440 | tf_op jit(solution)/shard_map/ppermute | solution.py:26
  153.4 1.4 copy-start.3
  156.7 96.8 %all-gather.11.cloned.1.call-start = ((), (), s32[]{:S(2)}) async-start(), calls=%async_computation.2 | async-start | bytes 1572864 | tf_op jit(solution)/shard_map/all_gather | solution.py:11
  167.2 1.2 copy-start.10
  168.3 0.9 copy-start.7
  226.2 13.7 %collective-permute-start.4 = (f32[1,256,256]{2,1,0:T(8,128)S(1)}, f32[1,256,256]{2,1,0:T(8,128)S(1)}, u32[]{:S(2)}, u32[]{:S(2)}) collective-permute-start(f32[1,256,256]{2,1,0:T(8,128)S(1)} %get-tuple-element.40), channel_id=1, source_target_pairs={{0,2},{2,4},{4,6},{6,8},{8,10},{10,12},{12,14},{14,16},{16,18},{18... | collective-permute-start | bytes 786440 | tf_op jit(solution)/shard_map/ppermute | solution.py:24
  230.4 11.3 %collective-permute-start.5 = (f32[1,256,256]{2,1,0:T(8,128)S(1)}, f32[1,256,256]{2,1,0:T(8,128)S(1)}, u32[]{:S(2)}, u32[]{:S(2)}) collective-permute-start(f32[1,256,256]{2,1,0:T(8,128)S(1)} %get-tuple-element.41), channel_id=1, source_target_pairs={{2,0},{4,2},{6,4},{8,6},{10,8},{12,10},{14,12},{16,14},{18,16},{20... | collective-permute-start | bytes 786440 | tf_op jit(solution)/shard_map/ppermute | solution.py:26
  241.8 1.4 copy-start.4
  255.7 1.2 copy-start.9
  255.7 1.4 copy-start.12
  256.9 1.7 copy-start.14
  257.0 57.7 %copy-start.13 = (f32[2,256,256]{2,1,0:T(8,128)S(1)}, f32[2,256,256]{2,1,0:T(8,128)}, u32[]{:S(2)}) copy-start(f32[2,256,256]{2,1,0:T(8,128)} %get-tuple-element.28) | copy-start | bytes 1572868
  314.8 3.5 %copy-start.15 = (f32[1,2,128,256]{3,2,1,0:T(8,128)S(1)}, f32[1,2,128,256]{3,2,1,0:T(8,128)}, u32[]{:S(2)}) copy-start(f32[1,2,128,256]{3,2,1,0:T(8,128)} %get-tuple-element.37) | copy-start | bytes 786436
Sparse Core Ops, SparseCore 0:
  72.6 8.1 all-gather.6
  156.8 8.1 all-gather.8
  245.3 8.1 all-gather.10
